TPU v7x, 32 devices: a whole 2x2x4 slice. The times are simulated.
32 devices in a mesh: row: 8 (over y, x, core), col: 4 (over z).
Axes of the slice: x: 2, y: 2, z: 4, core: 2. Of those that a mesh axis runs over, the one named last changes fastest.
Arguments:
- key_rows: float32 [128, 20480], P('col', 'row'), may hold values from -0.0390625 to 0.0390625
- targets: float32 [128, 7168], P(None, 'col'), may hold values from -24 to 24
- weight: float32 [20480, 7168], P('row', 'col'), may hold values from -6 to 6
- covariance: float32 [20480, 20480], P('row', 'col'), may hold values from -3 to 24, as said below
Outputs:
- increment: float32 [20480, 7168], P('row', 'col')
Inputs may be any that keep to these rules, and one draw needn't show every extreme that they name: covariance is symmetric and positive definite.
All inputs are finite; a program needn't handle non-finite values.
Results may differ from a plain program's by a relative error of at most 0.0003.
Values sent between devices are 32-bit elements; how exact they have to be, the bound alone decides.
No kernel may reach another device: no remote copies, remote signals or barrier semaphores. Data moves between devices by JAX's collectives and lax.ppermute only.
A program may use at most 192 MiB of HBM per device.

v0:
```python
import jax
import jax.numpy as jnp
from jax import lax
from jax.sharding import PartitionSpec as P


def spread(value, axis, root):
    mine = lax.axis_index(axis) == root
    return lax.psum(jnp.where(mine, value, jnp.zeros_like(value)), axis)


def precise(left, right):
    return jnp.dot(left, right, precision=lax.Precision.HIGHEST, preferred_element_type=jnp.float32)


def transposed_product(left, right):
    return lax.dot_general(
        left,
        right,
        (((0,), (0,)), ((), ())),
        precision=lax.Precision.HIGHEST,
        preferred_element_type=jnp.float32,
    )


def definite_solve(matrix, right_side):
    factor = jnp.linalg.cholesky(0.5 * (matrix + matrix.T))
    return jax.scipy.linalg.cho_solve((factor, True), right_side)


def fetch_panel(local_rows):
    blocks_per = lax.axis_size("row") // lax.axis_size("col")
    col_index = lax.axis_index("col")
    pieces = []
    for part_index in range(blocks_per):
        pieces.append(spread(local_rows, "row", col_index * blocks_per + part_index))
    return jnp.concatenate(pieces, axis=0)


def covariance_rows(covariance, local_rows):
    panel_rows = fetch_panel(local_rows)
    return lax.psum(precise(covariance, panel_rows), "col")


def body(key_rows, targets, weight, covariance):
    all_keys = lax.all_gather(key_rows, "col", axis=0, tiled=True)
    basis_panel = all_keys.T
    fitted, gram_keys = lax.psum((precise(all_keys, weight), precise(all_keys, basis_panel)), "row")
    residual = targets - fitted
    image_one = covariance_rows(covariance, basis_panel) + precise(basis_panel, gram_keys)
    curvature, square = lax.psum(
        (transposed_product(basis_panel, image_one), transposed_product(image_one, image_one)),
        "row",
    )
    alpha_one = definite_solve(curvature, gram_keys)
    residual_next = basis_panel - precise(image_one, alpha_one)
    norm_next = transposed_product(alpha_one, precise(square, alpha_one)) - gram_keys
    beta_one = definite_solve(gram_keys, norm_next)
    direction = residual_next + precise(basis_panel, beta_one)
    key_part = precise(all_keys, direction)
    cov_direction = covariance_rows(covariance, direction)
    key_direction, curve_part = lax.psum(
        (key_part, transposed_product(direction, cov_direction)), "row"
    )
    curvature_two = curve_part + transposed_product(key_direction, key_direction)
    alpha_two = definite_solve(curvature_two, norm_next)
    solved = precise(basis_panel, alpha_one) + precise(direction, alpha_two)
    return precise(solved, residual)


def solution(mesh):
    placed = (P("col", "row"), P(None, "col"), P("row", "col"), P("row", "col"))
    return jax.shard_map(
        body, mesh=mesh, in_specs=placed, out_specs=P("row", "col"), check_vma=False
    )
```

profile of v0, /device:TPU:0, one launch (start us, length us, event | category | flops | bytes accessed | tf_op | source)
XLA Modules:
  0.0 627.3 jit_solution(12307424067801751636)
XLA Ops:
  7.3 37.0 %all-gather.2.cloned.1.call-done = f32[128,2560]{1,0:T(8,128)} async-done(((f32[32,2560]{1,0:T(8,128)}), f32[128,2560]{1,0:T(8,128)}) %all-gather.2.cloned.1.call-update) | async-done | bytes 1310736 | tf_op jit(solution)/shard_map/all_gather | solution.py:46
  50.2 64.8 %all-reduce.21.cloned.1.call-done = (f32[128,128]{1,0:T(8,128)}, f32[2560,128]{1,0:T(8,128)}, f32[2560,128]{1,0:T(8,128)}) async-done(((f32[128,128]{1,0:T(8,128)}, f32[2560,128]{1,0:T(8,128)}, f32[2560,128]{1,0:T(8,128)}), (f32[128,128]{1,0:T(8,128)}, f32[2560,128]{1,0:T(8,128)}, f32[2560,128]{1,0:T(8,128)})) %all-reduce.21.cloned.1.call-update) | async-done | bytes 2686992 | tf_op jit(solution)/shard_map/psum | solution.py:48
  115.1 60.9 %convolution_bitcast_fusion.4 = f32[2560,128]{0,1:T(8,128)} fusion(f32[2560,5120]{1,0:T(8,128)} %param.10, f32[2560,128]{1,0:T(8,128)} %get-tuple-element.15, f32[2560,128]{1,0:T(8,128)} %get-tuple-element.16), kind=kOutput, calls=%fused_computation.8 | convolution fusion | flops 20133314560 | bytes 56360960 | tf_op jit(solution)/shard_map/dot_general | solution.py:13
  177.1 11.7 %cholesky.70 = f32[128,128]{1,0:T(8,128)S(1)} custom-call(f32[128,128]{1,0:T(8,128)S(1)} %fusion.23), custom_call_target="Cholesky" | custom-call | tf_op jit(solution)/shard_map/jit(cholesky)/cholesky | solution.py:27
  189.5 46.5 %all-reduce.11.cloned.1.call-done = f32[2560,128]{0,1:T(8,128)} async-done(((f32[2560,128]{0,1:T(8,128)}), f32[2560,128]{0,1:T(8,128)}) %all-reduce.11.cloned.1.call-update) | async-done | bytes 1310736 | tf_op jit(solution)/shard_map/psum | solution.py:42
  236.0 2.6 fusion.1
  243.4 9.8 %custom-call.10 = f32[1,128,128]{1,2,0:T(8,128)S(1)} custom-call(f32[1,128,128]{2,1,0:T(8,128)S(1)} %fusion.11), custom_call_target="InvertDiagBlocksLowerTriangular" | custom-call | tf_op jit(solution)/shard_map/jit(_cho_solve)/triangular_solve | solution.py:28
  253.2 42.0 %all-reduce.19.cloned.1.call-done = (f32[128,128]{1,0:T(8,128)}, f32[128,128]{1,0:T(8,128)}) async-done(((f32[128,128]{1,0:T(8,128)}, f32[128,128]{1,0:T(8,128)}), (f32[128,128]{1,0:T(8,128)}, f32[128,128]{1,0:T(8,128)})) %all-reduce.19.cloned.1.call-update) | async-done | bytes 131088 | tf_op jit(solution)/shard_map/psum | solution.py:51
  297.1 11.7 %cholesky.59 = f32[128,128]{1,0:T(8,128)S(1)} custom-call(f32[128,128]{1,0:T(8,128)S(1)} %fusion.29), custom_call_target="Cholesky" | custom-call | tf_op jit(solution)/shard_map/jit(cholesky)/cholesky | solution.py:27
  310.1 9.8 %custom-call.9 = f32[1,128,128]{1,2,0:T(8,128)S(1)} custom-call(f32[1,128,128]{2,1,0:T(8,128)S(1)} %fusion.10), custom_call_target="InvertDiagBlocksLowerTriangular" | custom-call | tf_op jit(solution)/shard_map/jit(_cho_solve)/triangular_solve | solution.py:28
  322.3 2.2 convolution_bitcast_fusion
  324.6 4.4 broadcast_select_fusion.1
  329.0 64.2 %all-reduce.17.cloned.1.call-done = (f32[2560,128]{1,0:T(8,128)}, f32[2560,128]{1,0:T(8,128)}) async-done(((f32[2560,128]{1,0:T(8,128)}, f32[2560,128]{1,0:T(8,128)}), (f32[2560,128]{1,0:T(8,128)}, f32[2560,128]{1,0:T(8,128)})) %all-reduce.17.cloned.1.call-update) | async-done | bytes 2621456 | tf_op jit(solution)/shard_map/psum | solution.py:9
  393.2 60.9 %convolution_bitcast_fusion.3 = f32[2560,128]{0,1:T(8,128)} fusion(f32[2560,5120]{1,0:T(8,128)} %param.10, f32[2560,128]{1,0:T(8,128)} %get-tuple-element.10, f32[2560,128]{1,0:T(8,128)} %get-tuple-element.11), kind=kOutput, calls=%fused_computation.7 | convolution fusion | flops 20133314560 | bytes 56360960 | tf_op jit(solution)/shard_map/dot_general | solution.py:13
  454.4 14.2 %fusion.37 = f32[128,1792]{1,0:T(8,128)} fusion(f32[128,2560]{1,0:T(8,128)S(1)} %copy-done, f32[2560,1792]{1,0:T(8,128)} %param.9), kind=kOutput, calls=%fused_computation.69 | convolution fusion | flops 7046430720 | bytes 20578304 | tf_op jit(solution)/shard_map/dot_general | solution.py:13
  468.6 2.9 convolution_bitcast_fusion.5
  471.5 42.5 %all-reduce.13.cloned.1.call-done = f32[2560,128]{0,1:T(8,128)} async-done(((f32[2560,128]{0,1:T(8,128)}), f32[2560,128]{0,1:T(8,128)}) %all-reduce.13.cloned.1.call-update) | async-done | bytes 1310736 | tf_op jit(solution)/shard_map/psum | solution.py:42
  514.0 4.2 fusion.36
  518.2 2.3 convolution_bitcast_fusion.1
  520.5 54.2 %all-reduce.15.cloned.1.call-done = (f32[128,128]{1,0:T(8,128)}, f32[128,128]{0,1:T(8,128)}, f32[128,1792]{1,0:T(8,128)}) async-done(((f32[128,128]{1,0:T(8,128)}, f32[128,128]{0,1:T(8,128)}, f32[128,1792]{1,0:T(8,128)}), (f32[128,128]{1,0:T(8,128)}, f32[128,128]{0,1:T(8,128)}, f32[128,1792]{1,0:T(8,128)})) %all-reduce.15.cloned.1.call-update) | async-done | bytes 1048592 | tf_op jit(solution)/shard_map/psum | solution.py:62
  576.2 11.7 %cholesky.81 = f32[128,128]{1,0:T(8,128)S(1)} custom-call(f32[128,128]{1,0:T(8,128)S(1)} %fusion.17), custom_call_target="Cholesky" | custom-call | tf_op jit(solution)/shard_map/jit(cholesky)/cholesky | solution.py:27
  589.2 9.8 %custom-call.11 = f32[1,128,128]{1,2,0:T(8,128)S(1)} custom-call(f32[1,128,128]{2,1,0:T(8,128)S(1)} %fusion.12), custom_call_target="InvertDiagBlocksLowerTriangular" | custom-call | tf_op jit(solution)/shard_map/jit(_cho_solve)/triangular_solve | solution.py:28
  599.8 2.8 convolution_add_fusion
  602.6 17.4 %fusion.8 = f32[2560,1792]{1,0:T(8,128)} fusion(f32[2560,128]{0,1:T(8,128)S(1)} %convolution_add_fusion, f32[128,1792]{1,0:T(8,128)S(1)} %copy-done.5, f32[128,1792]{1,0:T(8,128)S(1)} %copy-done.6), kind=kOutput, calls=%fused_computation.21 | convolution fusion | flops 7046660096 | bytes 21495808 | tf_op jit(solution)/shard_map/dot_general | solution.py:13
  (63 shorter events, 22.5 us)
Async XLA Ops:
  6.5 37.8 %all-gather.2.cloned.1.call-start = ((), (), s32[]{:S(2)}) async-start(), calls=%async_computation | async-start | bytes 1638400 | tf_op jit(solution)/shard_map/all_gather | solution.py:46
  7.3 107.8 %all-reduce.21.cloned.1.call-start = ((), (), s32[]{:S(2)}) async-start(), calls=%async_computation.6 | async-start | bytes 5373952 | tf_op jit(solution)/shard_map/psum | solution.py:48
  46.1 1.9 copy-start.2
  46.1 2.3 copy-start
  50.2 185.8 %all-reduce.11.cloned.1.call-start = ((), (), s32[]{:S(2)}) async-start(), calls=%async_computation.1 | async-start | bytes 2621440 | tf_op jit(solution)/shard_map/psum | solution.py:42
  176.0 0.8 copy-start.4
  176.0 119.2 %all-reduce.19.cloned.1.call-start = ((), (), s32[]{:S(2)}) async-start(), calls=%async_computation.5 | async-start | bytes 262144 | tf_op jit(solution)/shard_map/psum | solution.py:51
  242.2 151.0 %all-reduce.17.cloned.1.call-start = ((), (), s32[]{:S(2)}) async-start(), calls=%async_computation.4 | async-start | bytes 5242880 | tf_op jit(solution)/shard_map/psum | solution.py:9
  322.3 2.3 copy-start.3
  329.0 185.0 %all-reduce.13.cloned.1.call-start = ((), (), s32[]{:S(2)}) async-start(), calls=%async_computation.2 | async-start | bytes 2621440 | tf_op jit(solution)/shard_map/psum | solution.py:42
  454.2 14.4 %copy-start.1 = (f32[2560,128]{1,0:T(8,128)S(1)}, f32[2560,128]{1,0:T(8,128)}, u32[]{:S(2)}) copy-start(f32[2560,128]{1,0:T(8,128)} %get-tuple-element.21) | copy-start | bytes 3932164
  454.2 120.6 %all-reduce.15.cloned.1.call-start = ((), (), s32[]{:S(2)}) async-start(), calls=%async_computation.3 | async-start | bytes 2097152 | tf_op jit(solution)/shard_map/psum | solution.py:62
  599.8 2.8 copy-start.5
  599.8 2.8 copy-start.6
Sparse Core Ops, SparseCore 0:
  8.9 35.3 all-gather.1
  50.3 64.7 all-reduce.20
  176.1 59.7 all-reduce.10
  242.4 52.7 all-reduce.18
  329.1 64.0 all-reduce.16
  454.3 59.6 all-reduce.12
  518.3 56.3 all-reduce.14
where the time goes:
time: 637 us; the launch traced here: 627 us
  waiting for transfers between devices  352 us (55%)
  matrix products  184 us (29%)
  other arithmetic  71.3 us (11%)
  between operations  14.2 us (2%)
    dot_general x12, matrix products, precise(): jnp.dot(left, right, precision=lax.Precision.HIGHEST, preferred_element_t...  173 us
    psum x2, waiting for transfers between devices, covariance_rows(): return lax.psum(precise(covariance, panel_rows), 'col')  89 us
    psum x1, waiting for transfers between devices, body(): lax.psum((precise(all_keys, weight), precise(all_keys, basis_panel)), 'row')  64.8 us
    psum x1, waiting for transfers between devices, spread(): return lax.psum(jnp.where(mine, value, jnp.zeros_like(value)), axis)  64.2 us
    psum x1, waiting for transfers between devices, body(): lax.psum((key_part, transposed_product(direction, cov_direction)), 'row')  54.2 us
    psum x1, waiting for transfers between devices, body(): lax.psum((transposed_product(basis_panel, image_one), transposed_product(...  42 us
    another operation x9, other arithmetic, definite_solve(): factor = jnp.linalg.cholesky(0.5 * (matrix + matrix.T))  37.3 us
    all_gather x1, waiting for transfers between devices, body(): all_keys = lax.all_gather(key_rows, 'col', axis=0, tiled=True)  37 us
  transfers between devices with their start and end apart: 7, of which 7 were waited for; matrix products, arithmetic and copies ran while one was open for 7% of the time, Pallas kernels for 0%

commit v1 on v0

--- a/solution.py
+++ b/solution.py
@@ -6,7 +6,7 @@
 
 def spread(value, axis, root):
     mine = lax.axis_index(axis) == root
-    return lax.psum(jnp.where(mine, value, jnp.zeros_like(value)), axis)
+    return jnp.sum(lax.all_gather(jnp.where(mine, value, jnp.zeros_like(value)), axis), axis=0)
 
 
 def precise(left, right):

time: 637 us -> 767 us (1.20)
  waiting for transfers between devices: 352 us -> 466 us
  other arithmetic: 71.3 us -> 92.9 us
    all_gather x0 -> x4, waiting for transfers between devices: none -> 242 us  [spread(): lax.all_gather(jnp.where(mine, value, jnp.zeros_like(value)), axis)]
    psum x1, waiting for transfers between devices: 64.8 us -> 0.02 us  [body(): lax.psum((precise(all_keys, weight), precise(all_keys, basis_panel)), 'row')]
    psum x1 -> x0, waiting for transfers between devices: 64.2 us -> none  [spread(): return lax.psum(jnp.where(mine, value, jnp.zeros_like(value)), axis)]
    reduce_sum x0 -> x4, other arithmetic: none -> 20.6 us  [spread(): jnp.sum(lax.all_gather(jnp.where(mine, value, jnp.zeros_like(value)), axi...]
  transfers between devices with their start and end apart: 7 -> 10, of which waited for: 7 -> 9; matrix products, arithmetic and copies ran while one was open for 7% -> 16% of each run, Pallas kernels for 0% -> 0%
where the time goes in v1:
time: 767 us; the launch traced here: 764 us
  waiting for transfers between devices  466 us (61%)
  matrix products  185 us (24%)
  other arithmetic  92.9 us (12%)
  between operations  14.1 us (2%)
    all_gather x4, waiting for transfers between devices, spread(): lax.all_gather(jnp.where(mine, value, jnp.zeros_like(value)), axis)  242 us
    dot_general x12, matrix products, precise(): jnp.dot(left, right, precision=lax.Precision.HIGHEST, preferred_element_t...  174 us
    psum x2, waiting for transfers between devices, covariance_rows(): return lax.psum(precise(covariance, panel_rows), 'col')  88.1 us
    psum x1, waiting for transfers between devices, body(): lax.psum((key_part, transposed_product(direction, cov_direction)), 'row')  54.2 us
    psum x1, waiting for transfers between devices, body(): lax.psum((transposed_product(basis_panel, image_one), transposed_product(...  42.2 us
    another operation x9, other arithmetic, definite_solve(): factor = jnp.linalg.cholesky(0.5 * (matrix + matrix.T))  37.3 us
    all_gather x1, waiting for transfers between devices, body(): all_keys = lax.all_gather(key_rows, 'col', axis=0, tiled=True)  37 us
    another operation x6, other arithmetic, definite_solve(): return jax.scipy.linalg.cho_solve((factor, True), right_side)  31.4 us
  transfers between devices with their start and end apart: 10, of which 9 were waited for; matrix products, arithmetic and copies ran while one was open for 16% of the time, Pallas kernels for 0%

profile of v1, /device:TPU:0, one launch (start us, length us, event | category | flops | bytes accessed | tf_op | source)
XLA Modules:
  0.0 763.5 jit_solution(13931768302436963449)
XLA Ops:
  7.3 37.0 %all-gather.10.cloned.1.call-done = f32[128,2560]{1,0:T(8,128)} async-done(((f32[32,2560]{1,0:T(8,128)}), f32[128,2560]{1,0:T(8,128)}) %all-gather.10.cloned.1.call-update) | async-done | bytes 1310736 | tf_op jit(solution)/shard_map/all_gather | solution.py:46
  51.2 59.2 %all-gather.12.cloned.1.call-done = f32[20480,128]{1,0:T(8,128)} async-done(((f32[2560,128]{1,0:T(8,128)}), f32[20480,128]{1,0:T(8,128)}) %all-gather.12.cloned.1.call-update) | async-done | bytes 10485776 | tf_op jit(solution)/shard_map/all_gather | solution.py:9
  110.5 4.6 reduce_sum.36
  115.1 60.5 %all-gather.14.cloned.1.call-done = f32[20480,128]{1,0:T(8,128)} async-done(((f32[2560,128]{1,0:T(8,128)}), f32[20480,128]{1,0:T(8,128)}) %all-gather.14.cloned.1.call-update) | async-done | bytes 10485776 | tf_op jit(solution)/shard_map/all_gather | solution.py:9
  175.6 5.7 reduce_sum.37
  181.3 61.1 %convolution_bitcast_fusion.4 = f32[2560,128]{0,1:T(8,128)} fusion(f32[2560,5120]{1,0:T(8,128)} %param.10, f32[2560,128]{1,0:T(8,128)} %reduce_sum.37, f32[2560,128]{1,0:T(8,128)S(1)} %reduce_sum.36), kind=kOutput, calls=%fused_computation.8 | convolution fusion | flops 20133314560 | bytes 56360960 | tf_op jit(solution)/shard_map/dot_general | solution.py:13
  244.9 11.7 %cholesky.70 = f32[128,128]{1,0:T(8,128)S(1)} custom-call(f32[128,128]{1,0:T(8,128)S(1)} %fusion.23), custom_call_target="Cholesky" | custom-call | tf_op jit(solution)/shard_map/jit(cholesky)/cholesky | solution.py:27
  257.4 45.2 %all-reduce.8.cloned.1.call-done = f32[2560,128]{0,1:T(8,128)} async-done(((f32[2560,128]{0,1:T(8,128)}), f32[2560,128]{0,1:T(8,128)}) %all-reduce.8.cloned.1.call-update) | async-done | bytes 1310736 | tf_op jit(solution)/shard_map/psum | solution.py:42
  309.8 9.8 %custom-call.10 = f32[1,128,128]{1,2,0:T(8,128)S(1)} custom-call(f32[1,128,128]{2,1,0:T(8,128)S(1)} %fusion.11), custom_call_target="InvertDiagBlocksLowerTriangular" | custom-call | tf_op jit(solution)/shard_map/jit(_cho_solve)/triangular_solve | solution.py:28
  319.6 42.2 %all-reduce.16.cloned.1.call-done = (f32[128,128]{1,0:T(8,128)}, f32[128,128]{1,0:T(8,128)}) async-done(((f32[128,128]{1,0:T(8,128)}, f32[128,128]{1,0:T(8,128)}), (f32[128,128]{1,0:T(8,128)}, f32[128,128]{1,0:T(8,128)})) %all-reduce.16.cloned.1.call-update) | async-done | bytes 131088 | tf_op jit(solution)/shard_map/psum | solution.py:51
  363.7 11.7 %cholesky.59 = f32[128,128]{1,0:T(8,128)S(1)} custom-call(f32[128,128]{1,0:T(8,128)S(1)} %fusion.29), custom_call_target="Cholesky" | custom-call | tf_op jit(solution)/shard_map/jit(cholesky)/cholesky | solution.py:27
  376.8 9.8 %custom-call.9 = f32[1,128,128]{1,2,0:T(8,128)S(1)} custom-call(f32[1,128,128]{2,1,0:T(8,128)S(1)} %fusion.10), custom_call_target="InvertDiagBlocksLowerTriangular" | custom-call | tf_op jit(solution)/shard_map/jit(_cho_solve)/triangular_solve | solution.py:28
  391.3 4.6 broadcast_select_fusion.1
  396.7 62.0 %all-gather.16.cloned.1.call-done = f32[20480,128]{1,0:T(8,128)} async-done(((f32[2560,128]{1,0:T(8,128)}), f32[20480,128]{1,0:T(8,128)}) %all-gather.16.cloned.1.call-update) | async-done | bytes 10485776 | tf_op jit(solution)/shard_map/all_gather | solution.py:9
  458.7 4.6 reduce_sum.38
  463.3 60.5 %all-gather.18.cloned.1.call-done = f32[20480,128]{1,0:T(8,128)} async-done(((f32[2560,128]{1,0:T(8,128)}), f32[20480,128]{1,0:T(8,128)}) %all-gather.18.cloned.1.call-update) | async-done | bytes 10485776 | tf_op jit(solution)/shard_map/all_gather | solution.py:9
  523.8 5.7 reduce_sum.39
  529.5 60.8 %convolution_bitcast_fusion.3 = f32[2560,128]{0,1:T(8,128)} fusion(f32[2560,5120]{1,0:T(8,128)} %param.10, f32[2560,128]{1,0:T(8,128)} %reduce_sum.39, f32[2560,128]{1,0:T(8,128)S(1)} %reduce_sum.38), kind=kOutput, calls=%fused_computation.7 | convolution fusion | flops 20133314560 | bytes 56360960 | tf_op jit(solution)/shard_map/dot_general | solution.py:13
  590.4 14.3 %fusion.37 = f32[128,1792]{1,0:T(8,128)} fusion(f32[128,2560]{1,0:T(8,128)S(1)} %copy-done, f32[2560,1792]{1,0:T(8,128)} %param.9), kind=kOutput, calls=%fused_computation.69 | convolution fusion | flops 7046430720 | bytes 20578304 | tf_op jit(solution)/shard_map/dot_general | solution.py:13
  607.6 42.9 %all-reduce.12.cloned.1.call-done = f32[2560,128]{0,1:T(8,128)} async-done(((f32[2560,128]{0,1:T(8,128)}), f32[2560,128]{0,1:T(8,128)}) %all-reduce.12.cloned.1.call-update) | async-done | bytes 1310736 | tf_op jit(solution)/shard_map/psum | solution.py:42
  657.0 54.2 %all-reduce.14.cloned.1.call-done = (f32[128,128]{1,0:T(8,128)}, f32[128,128]{0,1:T(8,128)}, f32[128,1792]{1,0:T(8,128)}) async-done(((f32[128,128]{1,0:T(8,128)}, f32[128,128]{0,1:T(8,128)}, f32[128,1792]{1,0:T(8,128)}), (f32[128,128]{1,0:T(8,128)}, f32[128,128]{0,1:T(8,128)}, f32[128,1792]{1,0:T(8,128)})) %all-reduce.14.cloned.1.call-update) | async-done | bytes 1048592 | tf_op jit(solution)/shard_map/psum | solution.py:62
  712.6 11.7 %cholesky.81 = f32[128,128]{1,0:T(8,128)S(1)} custom-call(f32[128,128]{1,0:T(8,128)S(1)} %fusion.17), custom_call_target="Cholesky" | custom-call | tf_op jit(solution)/shard_map/jit(cholesky)/cholesky | solution.py:27
  725.7 9.8 %custom-call.11 = f32[1,128,128]{1,2,0:T(8,128)S(1)} custom-call(f32[1,128,128]{2,1,0:T(8,128)S(1)} %fusion.12), custom_call_target="InvertDiagBlocksLowerTriangular" | custom-call | tf_op jit(solution)/shard_map/jit(_cho_solve)/triangular_solve | solution.py:28
  739.0 17.4 %fusion.8 = f32[2560,1792]{1,0:T(8,128)} fusion(f32[2560,128]{0,1:T(8,128)S(1)} %convolution_add_fusion, f32[128,1792]{1,0:T(8,128)S(1)} %copy-done.5, f32[128,1792]{1,0:T(8,128)S(1)} %copy-done.6), kind=kOutput, calls=%fused_computation.21 | convolution fusion | flops 7046660096 | bytes 21495808 | tf_op jit(solution)/shard_map/dot_general | solution.py:13
  (76 shorter events, 42.1 us)
Async XLA Ops:
  6.5 37.8 %all-gather.10.cloned.1.call-start = ((), (), s32[]{:S(2)}) async-start(), calls=%async_computation | async-start | bytes 1638400 | tf_op jit(solution)/shard_map/all_gather | solution.py:46
  7.3 103.2 %all-gather.12.cloned.1.call-start = ((), (), s32[]{:S(2)}) async-start(), calls=%async_computation.4 | async-start | bytes 11796480 | tf_op jit(solution)/shard_map/all_gather | solution.py:9
  46.1 2.0 copy-start.2
  48.0 1.3 copy-start
  48.1 127.6 %all-gather.14.cloned.1.call-start = ((), (), s32[]{:S(2)}) async-start(), calls=%async_computation.5 | async-start | bytes 11796480 | tf_op jit(solution)/shard_map/all_gather | solution.py:9
  48.8 194.2 %all-reduce.10.cloned.1.call-start = ((), (), s32[]{:S(2)}) async-start(), calls=%async_computation.2 | async-start | bytes 131072 | tf_op jit(solution)/shard_map/psum | solution.py:48
  51.2 251.4 %all-reduce.8.cloned.1.call-start = ((), (), s32[]{:S(2)}) async-start(), calls=%async_computation.1 | async-start | bytes 2621440 | tf_op jit(solution)/shard_map/psum | solution.py:42
  242.4 119.4 %all-reduce.16.cloned.1.call-start = ((), (), s32[]{:S(2)}) async-start(), calls=%async_computation.9 | async-start | bytes 262144 | tf_op jit(solution)/shard_map/psum | solution.py:51
  307.0 79.6 %copy-start.4 = (f32[128,128]{1,0:T(8,128)S(1)}, f32[128,128]{1,0:T(8,128)}, u32[]{:S(2)}) copy-start(f32[128,128]{1,0:T(8,128)} %all-reduce.10.cloned.1.call-done) | copy-start | bytes 196612
  308.9 149.8 %all-gather.16.cloned.1.call-start = ((), (), s32[]{:S(2)}) async-start(), calls=%async_computation.6 | async-start | bytes 11796480 | tf_op jit(solution)/shard_map/all_gather | solution.py:9
  389.0 2.3 copy-start.3
  395.9 127.9 %all-gather.18.cloned.1.call-start = ((), (), s32[]{:S(2)}) async-start(), calls=%async_computation.7 | async-start | bytes 11796480 | tf_op jit(solution)/shard_map/all_gather | solution.py:9
  396.7 253.8 %all-reduce.12.cloned.1.call-start = ((), (), s32[]{:S(2)}) async-start(), calls=%async_computation.3 | async-start | bytes 2621440 | tf_op jit(solution)/shard_map/psum | solution.py:42
  590.3 14.4 %copy-start.1 = (f32[2560,128]{1,0:T(8,128)S(1)}, f32[2560,128]{1,0:T(8,128)}, u32[]{:S(2)}) copy-start(f32[2560,128]{1,0:T(8,128)} %get-tuple-element.16) | copy-start | bytes 3932164
  590.3 120.9 %all-reduce.14.cloned.1.call-start = ((), (), s32[]{:S(2)}) async-start(), calls=%async_computation.8 | async-start | bytes 2097152 | tf_op jit(solution)/shard_map/psum | solution.py:62
  736.2 2.8 copy-start.5
  736.2 2.8 copy-start.6
Sparse Core Ops, SparseCore 0:
  8.9 35.3 all-gather.9
  48.2 62.2 all-gather.11
  112.3 63.2 all-gather.13
  178.5 52.4 all-reduce.9
  242.5 60.0 all-reduce.7
  309.0 52.7 all-reduce.15
  396.0 62.6 all-gather.15
  460.6 63.2 all-gather.17
  590.5 59.9 all-reduce.11
  654.8 56.3 all-reduce.13
